TPU v7x, 32 devices: a whole 2x2x4 slice. The times are simulated.
32 devices in a mesh: fibre: 4 (over z), cols: 8 (over y, x, core).
Axes of the slice: x: 2, y: 2, z: 4, core: 2. Of those that a mesh axis runs over, the one named last changes fastest.
Arguments:
- tensor: float32 [512, 8, 4, 2048], P('fibre', 'cols'), may hold values from -6 to 6
- initial: float32 [512, 64], replicated, may hold values from -6 to 6
Outputs:
- core_slab: float32 [64, 8, 4, 2048], P(None, 'cols', 'fibre')
- basis: float32 [512, 64], replicated
All inputs are finite; a program needn't handle non-finite values.
Results may differ from a plain program's by a relative error of at most 0.0002.
Values sent between devices are 32-bit elements; how exact they have to be, the bound alone decides.
No kernel may reach another device: no remote copies, remote signals or barrier semaphores. Data moves between devices by JAX's collectives and lax.ppermute only.
A program may use at most 64 MiB of HBM per device.

v0:
```python
import jax
import jax.numpy as jnp
from jax import lax
from jax.sharding import PartitionSpec as P

ITERS = 2


def orthonormal(product):
    squares = jnp.dot(product.T, product, precision=lax.Precision.HIGHEST)
    lower = jnp.linalg.cholesky(squares)
    return lax.linalg.triangular_solve(
        lower, product, left_side=False, lower=True, transpose_a=True
    )


def shards(tensor, initial):
    highest = lax.Precision.HIGHEST
    gathered = lax.all_to_all(tensor, "fibre", split_axis=2, concat_axis=0, tiled=True)
    modes = gathered.shape[0]
    width = gathered.shape[3]
    columns = gathered.reshape(modes, width)
    local_gram = jnp.dot(columns, columns.T, precision=highest)
    gram = lax.psum(local_gram, ("fibre", "cols"))
    basis = initial
    for step in range(ITERS):
        basis = orthonormal(jnp.dot(gram, basis, precision=highest))
    ranks = basis.shape[1]
    core_slab = jnp.dot(basis.T, columns, precision=highest).reshape(ranks, 1, 1, width)
    return (core_slab, basis)


def solution(mesh):
    placed = (P("fibre", "cols", None, None), P())
    return jax.shard_map(
        shards,
        mesh=mesh,
        in_specs=placed,
        out_specs=(P(None, "cols", "fibre", None), P()),
        check_vma=False,
    )
```

profile of v0, /device:TPU:0, one launch (start us, length us, event | category | flops | bytes accessed | tf_op | source)
XLA Modules:
  0.0 294.8 jit_solution(3393844328094002086)
XLA Ops:
  7.2 0.0 all-reduce.2.cloned.1.call-start
  7.2 4.6 %copy.11 = f32[128,1,4,2048]{3,0,1,2:T(8,128)S(1)} copy(f32[128,1,4,2048]{3,2,1,0:T(4,128)} %param.5) | data formatting | bytes 8388608 | tf_op args[0]
  11.9 99.3 %all_to_all.15 = f32[128,1,4,2048]{3,0,1,2:T(8,128)S(1)} all-to-all(f32[128,1,4,2048]{3,0,1,2:T(8,128)S(1)} %copy.11), channel_id=1, replica_groups=mesh['fibre'=4,'cols'=8] {'fibre'}, dimensions={2} | all-to-all | bytes 8388608 | tf_op jit(solution)/shard_map/all_to_all | solution.py:19
  111.2 1.9 copy-done.1
  113.1 7.9 %fusion.8 = f32[512,512]{1,0:T(8,128)} fusion(f32[512,2048]{1,0:T(8,128)S(1)} %bitcast.43), kind=kOutput, calls=%fused_computation.20 | convolution fusion | flops 6442450944 | bytes 5242880 | tf_op jit(solution)/shard_map/dot_general | solution.py:23
  121.0 130.2 %all-reduce.2.cloned.1.call-done = f32[512,512]{1,0:T(8,128)} async-done(((f32[512,512]{1,0:T(8,128)}), f32[512,512]{1,0:T(8,128)}) %all-reduce.2.cloned.1.call-update) | async-done | bytes 1048592 | tf_op jit(solution)/shard_map/psum | solution.py:24
  251.3 2.4 fusion.9
  253.6 0.3 fusion.10
  253.9 0.1 copy.12
  254.0 5.8 %cholesky.44 = f32[64,64]{1,0:T(8,128)S(1)} custom-call(f32[64,64]{1,0:T(8,128)S(1)} %fusion.5), custom_call_target="Cholesky" | custom-call | tf_op jit(solution)/shard_map/jit(cholesky)/cholesky | solution.py:11
  259.9 0.6 compare_reduce_fusion.1
  260.5 0.7 fusion
  261.2 4.9 %custom-call.6 = f32[1,64,64]{1,2,0:T(8,128)S(1)} custom-call(f32[1,64,64]{2,1,0:T(8,128)S(1)} %fusion), custom_call_target="InvertDiagBlocksLowerTriangular" | custom-call | tf_op jit(solution)/shard_map/triangular_solve/custom-call.0 | solution.py:12
  266.1 0.3 convolution_bitcast_fusion.2
  266.4 2.4 fusion.11
  268.8 0.3 fusion.12
  269.0 0.1 copy.13
  269.1 6.0 %cholesky.55 = f32[64,64]{1,0:T(8,128)S(1)} custom-call(f32[64,64]{1,0:T(8,128)S(1)} %fusion.3), custom_call_target="Cholesky" | custom-call | tf_op jit(solution)/shard_map/jit(cholesky)/cholesky | solution.py:11
  275.2 0.6 compare_reduce_fusion
  275.8 0.7 fusion.1
  276.5 4.9 %custom-call.7 = f32[1,64,64]{1,2,0:T(8,128)S(1)} custom-call(f32[1,64,64]{2,1,0:T(8,128)S(1)} %fusion.1), custom_call_target="InvertDiagBlocksLowerTriangular" | custom-call | tf_op jit(solution)/shard_map/triangular_solve/custom-call.0 | solution.py:12
  281.4 0.3 convolution_bitcast_fusion.1
  281.8 4.9 %convolution_bitcast_fusion = f32[64,1,1,2048]{3,0,2,1:T(8,128)S(1)} fusion(f32[512,64]{0,1:T(8,128)S(1)} %convolution_bitcast_fusion.1, f32[512,2048]{1,0:T(8,128)} %bitcast.44), kind=kOutput, calls=%fused_computation | convolution fusion | flops 805306368 | bytes 4849664 | tf_op jit(solution)/shard_map/dot_general | solution.py:29
  286.6 1.3 copy.14
  (10 shorter events, 0.1 us)
Async XLA Ops:
  7.2 244.1 %copy-start = (f32[512,64]{0,1:T(8,128)S(1)}, f32[512,64]{0,1:T(8,128)}, u32[]{:S(2)}) copy-start(f32[512,64]{0,1:T(8,128)} %param.6) | copy-start | bytes 393220
  7.2 244.1 %all-reduce.2.cloned.1.call-start = ((), (), s32[]{:S(2)}) async-start(), calls=%async_computation.1 | async-start | bytes 2097152 | tf_op jit(solution)/shard_map/psum | solution.py:24
  111.2 1.9 copy-start.1
  281.7 6.2 %copy-start.2 = (f32[512,64]{0,1:T(8,128)}, f32[512,64]{0,1:T(8,128)S(1)}, u32[]{:S(2)}) copy-start(f32[512,64]{0,1:T(8,128)S(1)} %convolution_bitcast_fusion.1) | copy-start | bytes 393220
Sparse Core Ops, SparseCore 0:
  121.2 130.0 all-reduce.1
where the time goes:
time: 295 us
  waiting for transfers between devices  130 us (44%)
  blocking collectives  99.3 us (34%)
  other arithmetic  24.4 us (8%)
  matrix products  18.7 us (6%)
  between operations  14.1 us (5%)
  local copies, waits for them, and re-layouts  8.07 us (3%)
    psum x1, waiting for transfers between devices, shards(): gram = lax.psum(local_gram, ('fibre', 'cols'))  130 us
    all_to_all x1, blocking collectives, shards(): lax.all_to_all(tensor, 'fibre', split_axis=2, concat_axis=0, tiled=True)  99.3 us
    another operation x6, other arithmetic, orthonormal(): lower = jnp.linalg.cholesky(squares)  13.2 us
    another operation x4, other arithmetic, orthonormal(): lax.linalg.triangular_solve(lower, product, left_side=False, lower=True,...  11.1 us
    dot_general x1, matrix products, shards(): local_gram = jnp.dot(columns, columns.T, precision=highest)  7.93 us
    unnamed x8, local copies, waits for them, and re-layouts  7.92 us
  transfers between devices with their start and end apart: 1, of which 1 were waited for; matrix products, arithmetic and copies ran while one was open for 0% of the time, Pallas kernels for 0%

commit v1 on v0

--- a/solution.py
+++ b/solution.py
@@ -21,7 +21,7 @@
     width = gathered.shape[3]
     columns = gathered.reshape(modes, width)
     local_gram = jnp.dot(columns, columns.T, precision=highest)
-    gram = lax.psum(local_gram, ("fibre", "cols"))
+    gram = lax.psum(lax.psum(local_gram, "cols"), "fibre")
     basis = initial
     for step in range(ITERS):
         basis = orthonormal(jnp.dot(gram, basis, precision=highest))

time: 295 us -> 274 us (0.929)
  waiting for transfers between devices: 130 us -> 110 us
    psum x1 -> x2, waiting for transfers between devices: 130 us -> 109 us  [shards(): gram = lax.psum(lax.psum(local_gram, 'cols'), 'fibre')]
  transfers between devices with their start and end apart: 1 -> 2, of which waited for: 1 -> 2; matrix products, arithmetic and copies ran while one was open for 0% -> 0% of each run, Pallas kernels for 0% -> 0%
where the time goes in v1:
time: 274 us
  waiting for transfers between devices  110 us (40%)
  blocking collectives  99.3 us (36%)
  other arithmetic  24.2 us (9%)
  matrix products  18.7 us (7%)
  between operations  14.1 us (5%)
  local copies, waits for them, and re-layouts  8.07 us (3%)
    psum x2, waiting for transfers between devices, shards(): gram = lax.psum(lax.psum(local_gram, 'cols'), 'fibre')  109 us
    all_to_all x1, blocking collectives, shards(): lax.all_to_all(tensor, 'fibre', split_axis=2, concat_axis=0, tiled=True)  99.3 us
    another operation x6, other arithmetic, orthonormal(): lower = jnp.linalg.cholesky(squares)  13 us
    another operation x4, other arithmetic, orthonormal(): lax.linalg.triangular_solve(lower, product, left_side=False, lower=True,...  11.1 us
    dot_general x1, matrix products, shards(): local_gram = jnp.dot(columns, columns.T, precision=highest)  7.93 us
    unnamed x8, local copies, waits for them, and re-layouts  7.92 us
  transfers between devices with their start and end apart: 2, of which 2 were waited for; matrix products, arithmetic and copies ran while one was open for 0% of the time, Pallas kernels for 0%

profile of v1, /device:TPU:0, one launch (start us, length us, event | category | flops | bytes accessed | tf_op | source)
XLA Modules:
  0.0 274.1 jit_solution(10527738758736755894)
XLA Ops:
  7.2 4.6 %copy.11 = f32[128,1,4,2048]{3,0,1,2:T(8,128)S(1)} copy(f32[128,1,4,2048]{3,2,1,0:T(4,128)} %param.5) | data formatting | bytes 8388608 | tf_op args[0]
  11.9 99.3 %all_to_all.15 = f32[128,1,4,2048]{3,0,1,2:T(8,128)S(1)} all-to-all(f32[128,1,4,2048]{3,0,1,2:T(8,128)S(1)} %copy.11), channel_id=1, replica_groups=mesh['fibre'=4,'cols'=8] {'fibre'}, dimensions={2} | all-to-all | bytes 8388608 | tf_op jit(solution)/shard_map/all_to_all | solution.py:19
  111.2 1.9 copy-done.1
  113.1 7.9 %fusion.8 = f32[512,512]{1,0:T(8,128)} fusion(f32[512,2048]{1,0:T(8,128)S(1)} %bitcast.43), kind=kOutput, calls=%fused_computation.20 | convolution fusion | flops 6442450944 | bytes 5242880 | tf_op jit(solution)/shard_map/dot_general | solution.py:23
  121.0 0.2 all-reduce.5.cloned.1.call-start
  121.3 56.0 %all-reduce.3.cloned.1.call-done = f32[512,512]{1,0:T(8,128)} async-done(((f32[512,512]{1,0:T(8,128)}), f32[512,512]{1,0:T(8,128)}) %all-reduce.3.cloned.1.call-update) | async-done | bytes 1048592 | tf_op jit(solution)/shard_map/psum | solution.py:24
  177.3 53.5 %all-reduce.5.cloned.1.call-done = f32[512,512]{1,0:T(8,128)} async-done(((f32[512,512]{1,0:T(8,128)}), f32[512,512]{1,0:T(8,128)}) %all-reduce.5.cloned.1.call-update) | async-done | bytes 1048592 | tf_op jit(solution)/shard_map/psum | solution.py:24
  230.8 2.4 fusion.9
  233.1 0.3 fusion.10
  233.4 0.1 copy.12
  233.5 5.8 %cholesky.44 = f32[64,64]{1,0:T(8,128)S(1)} custom-call(f32[64,64]{1,0:T(8,128)S(1)} %fusion.5), custom_call_target="Cholesky" | custom-call | tf_op jit(solution)/shard_map/jit(cholesky)/cholesky | solution.py:11
  239.4 0.6 compare_reduce_fusion.1
  240.0 0.7 fusion
  240.7 4.9 %custom-call.6 = f32[1,64,64]{1,2,0:T(8,128)S(1)} custom-call(f32[1,64,64]{2,1,0:T(8,128)S(1)} %fusion), custom_call_target="InvertDiagBlocksLowerTriangular" | custom-call | tf_op jit(solution)/shard_map/triangular_solve/custom-call.0 | solution.py:12
  245.6 0.3 convolution_bitcast_fusion.2
  245.9 2.4 fusion.11
  248.3 0.3 fusion.12
  248.6 5.8 %cholesky.55 = f32[64,64]{1,0:T(8,128)S(1)} custom-call(f32[64,64]{1,0:T(8,128)S(1)} %fusion.3), custom_call_target="Cholesky" | custom-call | tf_op jit(solution)/shard_map/jit(cholesky)/cholesky | solution.py:11
  254.5 0.6 compare_reduce_fusion
  255.2 0.7 fusion.1
  255.8 4.9 %custom-call.7 = f32[1,64,64]{1,2,0:T(8,128)S(1)} custom-call(f32[1,64,64]{2,1,0:T(8,128)S(1)} %fusion.1), custom_call_target="InvertDiagBlocksLowerTriangular" | custom-call | tf_op jit(solution)/shard_map/triangular_solve/custom-call.0 | solution.py:12
  260.7 0.3 convolution_bitcast_fusion.1
  261.1 4.9 %convolution_bitcast_fusion = f32[64,1,1,2048]{3,0,2,1:T(8,128)S(1)} fusion(f32[512,64]{0,1:T(8,128)S(1)} %convolution_bitcast_fusion.1, f32[512,2048]{1,0:T(8,128)} %bitcast.44), kind=kOutput, calls=%fused_computation | convolution fusion | flops 805306368 | bytes 4849664 | tf_op jit(solution)/shard_map/dot_general | solution.py:29
  265.9 1.3 copy.14
  (13 shorter events, 0.2 us)
Async XLA Ops:
  7.2 223.6 %copy-start = (f32[512,64]{0,1:T(8,128)S(1)}, f32[512,64]{0,1:T(8,128)}, u32[]{:S(2)}) copy-start(f32[512,64]{0,1:T(8,128)} %param.6) | copy-start | bytes 393220
  7.2 170.1 %all-reduce.3.cloned.1.call-start = ((), (), s32[]{:S(2)}) async-start(), calls=%async_computation.1 | async-start | bytes 2097152 | tf_op jit(solution)/shard_map/psum | solution.py:24
  111.2 1.9 copy-start.1
  121.0 109.7 %all-reduce.5.cloned.1.call-start = ((), (), s32[]{:S(2)}) async-start(), calls=%async_computation.2 | async-start | bytes 2097152 | tf_op jit(solution)/shard_map/psum | solution.py:24
  261.1 6.2 %copy-start.2 = (f32[512,64]{0,1:T(8,128)}, f32[512,64]{0,1:T(8,128)S(1)}, u32[]{:S(2)}) copy-start(f32[512,64]{0,1:T(8,128)S(1)} %convolution_bitcast_fusion.1) | copy-start | bytes 393220
Sparse Core Ops, SparseCore 0:
  121.2 56.0 all-reduce.2
  179.6 51.1 all-reduce.4
